TPU v7x, 32 devices: a whole 2x2x4 slice. The times are simulated.
32 devices in a mesh: gx: 4 (over x, core), gy: 8 (over z, y).
Axes of the slice: x: 2, y: 2, z: 4, core: 2. Of those that a mesh axis runs over, the one named last changes fastest.
Arguments:
- increment: float32 [8, 2048, 1024], P(None, 'gx', 'gy'), may hold values from -6 to 6
- deviation: float32 [8, 2048, 1024], P(None, 'gx', 'gy'), may hold values from 0.5 to 2
- land_sea: int32 [8, 2048, 1024], P(None, 'gx', 'gy'), may hold values 0 or 1
- filter_steps: int32 [8], replicated, may hold values from 1 to 2, as said below
- zonal_rate: float32 [8], replicated, may hold values from 0.0009765625 to 0.03
- meridional_rate: float32 [8], replicated, may hold values from 0.001953125 to 0.03
Outputs:
- covaried: float32 [8, 2048, 1024], P(None, 'gx', 'gy')
Inputs may be any that keep to these rules, and one draw needn't show every extreme that they name: `filter_steps`: some level has 2 repetitions and some level has 1.
All inputs are finite; a program needn't handle non-finite values. No bound on the sum of `land_sea` on one device may be relied on, other than what follows from the above.
Results may differ from a plain program's by a relative error of at most 0.0003.
Values sent between devices are 32-bit elements; how exact they have to be, the bound alone decides.
A program may use at most 128 MiB of HBM per device.

v0:
```python
import jax
import jax.numpy as jnp
from jax import lax
from jax.sharding import PartitionSpec as P

BLOCK = 128
MAXSTEPS = 2


gain_base = 3.0**0.125
highest = lax.Precision.HIGHEST


def section_gain(decay_rate, filter_steps):
    fading = -jnp.expm1(-decay_rate)
    return gain_base * fading ** (1.0 - 1.0 / (16.0 * filter_steps.astype(jnp.float32)))


def transfer(decay_rate, section_weight, span):
    orders = jnp.arange(4)
    offset = (orders[:, None] - orders[None, :]).astype(jnp.float32)
    count = span[None, ..., None, None]
    extra = len(span.shape) + 2
    rates = decay_rate.reshape((-1,) + (1,) * extra)
    weights = section_weight.reshape((-1,) + (1,) * extra)
    binomial = jnp.where(
        offset < 0.5,
        1.0,
        jnp.where(
            offset < 1.5,
            count,
            jnp.where(
                offset < 2.5,
                count * (count + 1.0) / 2.0,
                count * (count + 1.0) * (count + 2.0) / 6.0,
            ),
        ),
    )
    return jnp.where(
        offset > -0.5, jnp.exp(-rates * count) * weights ** jnp.maximum(offset, 0.0) * binomial, 0.0
    )


def block_tables(decay_rate, section_weight, backward):
    places = jnp.arange(BLOCK).astype(jnp.float32)
    lagged = places[:, None] - places[None, :]
    span = jnp.maximum(lagged, 0.0)
    rates = decay_rate[:, None, None]
    weights = section_weight[:, None, None]
    tile = jnp.where(
        lagged > -0.5,
        weights**4 * jnp.exp(-rates * span) * (span + 1.0) * (span + 2.0) * (span + 3.0) / 6.0,
        0.0,
    )
    remain = BLOCK - 1.0 - places
    orders = jnp.arange(4).astype(jnp.float32)[:, None]
    binomial = jnp.where(
        orders < 0.5,
        1.0,
        jnp.where(
            orders < 1.5,
            remain + 1.0,
            jnp.where(
                orders < 2.5,
                (remain + 1.0) * (remain + 2.0) / 2.0,
                (remain + 1.0) * (remain + 2.0) * (remain + 3.0) / 6.0,
            ),
        ),
    )
    finals = weights ** (orders + 1.0)[None] * jnp.exp(-rates * remain) * binomial[None]
    response = transfer(decay_rate, section_weight, places + 1.0)[:, :, 3, :]
    if backward:
        tile = tile[:, ::-1, ::-1]
        finals = finals[:, :, ::-1]
        response = response[:, ::-1, :]
    return (tile, finals, response)


def remote_sum(pieces, anchor, own_index, decay_rate, section_weight, device_span, backward):
    if backward:
        distance = anchor - 1 - own_index
    else:
        distance = own_index - 1 - anchor
    reach = (device_span * jnp.maximum(distance, 0)).astype(jnp.float32)
    mixing = transfer(decay_rate, section_weight, reach)
    mixing = jnp.where((distance >= 0)[None, :, None, None], mixing, 0.0)
    return jnp.einsum("ljkm,jlmw->lkw", mixing, pieces, precision=highest)


def device_carry(device_end, decay_rate, section_weight, device_span, zonal, backward):
    if zonal:
        pieces = lax.all_gather(device_end[None], "gx", axis=0, tiled=True)
        own_index = lax.axis_index("gx")
    else:
        pieces = lax.all_gather(device_end[None], "gy", axis=0, tiled=True)
        own_index = lax.axis_index("gy")
    anchor = jnp.arange(pieces.shape[0])
    return remote_sum(pieces, anchor, own_index, decay_rate, section_weight, device_span, backward)


def filter_pass(field, decay_rate, section_weight, zonal, backward):
    tile, finals, response = block_tables(decay_rate, section_weight, backward)
    levels, rows_here, cols_here = field.shape
    if zonal:
        blocks = rows_here // BLOCK
        shaped = field.reshape(levels, blocks, BLOCK, cols_here)
        inside = jnp.einsum("lpq,lbqw->lbpw", tile, shaped, precision=highest)
        closing = jnp.einsum("lkq,lbqw->lbkw", finals, shaped, precision=highest)
    else:
        blocks = cols_here // BLOCK
        shaped = field.reshape(levels, rows_here, blocks, BLOCK)
        inside = jnp.einsum("lpq,lwbq->lwbp", tile, shaped, precision=highest)
        closing = jnp.einsum("lkq,lwbq->lbkw", finals, shaped, precision=highest)
    sources = jnp.arange(blocks)
    if backward:
        targets = jnp.arange(blocks + 1) - 1
        distance = sources[None, :] - 1 - targets[:, None]
    else:
        targets = jnp.arange(blocks + 1)
        distance = targets[:, None] - 1 - sources[None, :]
    mixing = transfer(
        decay_rate, section_weight, (BLOCK * jnp.maximum(distance, 0)).astype(jnp.float32)
    )
    mixing = jnp.where((distance >= 0)[None, :, :, None, None], mixing, 0.0)
    inward = jnp.einsum("ltskm,lsmw->ltkw", mixing, closing, precision=highest)
    if backward:
        device_end = inward[:, 0]
        block_start = inward[:, 1:]
        ranks = blocks - 1 - sources
    else:
        device_end = inward[:, blocks]
        block_start = inward[:, :blocks]
        ranks = sources
    device_span = BLOCK * blocks
    carried = device_carry(device_end, decay_rate, section_weight, device_span, zonal, backward)
    spread = transfer(decay_rate, section_weight, (BLOCK * ranks).astype(jnp.float32))
    block_start = block_start + jnp.einsum("lbkm,lmw->lbkw", spread, carried, precision=highest)
    if zonal:
        result = inside + jnp.einsum("lpk,lbkw->lbpw", response, block_start, precision=highest)
    else:
        result = inside + jnp.einsum("lpk,lbkw->lwbp", response, block_start, precision=highest)
    return result.reshape(levels, rows_here, cols_here)


def on_device(increment, deviation, land_sea, filter_steps, zonal_rate, meridional_rate):
    wetness = land_sea.astype(jnp.float32)
    field = deviation * wetness * increment
    for repeat in range(MAXSTEPS):
        active = (filter_steps > repeat)[:, None, None]
        current = field
        for zonal, rates in ((True, zonal_rate), (False, meridional_rate)):
            weights = section_gain(rates, filter_steps)
            current = wetness * filter_pass(current, rates, weights, zonal, False)
            current = wetness * filter_pass(current, rates, weights, zonal, True)
        field = jnp.where(active, current, field)
    return deviation * field


def solution(mesh):
    placed = (P(None, "gx", "gy"), P(None, "gx", "gy"), P(None, "gx", "gy"), P(), P(), P())
    return jax.shard_map(
        on_device, mesh=mesh, in_specs=placed, out_specs=P(None, "gx", "gy"), check_vma=False
    )
```

profile of v0, /device:TPU:0, one launch (start us, length us, event | category | flops | bytes accessed | tf_op | source)
XLA Modules:
  0.0 267.8 jit_solution(93494451590781796)
XLA Ops:
  0.0 3.2 %multiply_multiply_fusion = f32[8,512,128]{2,1,0:T(8,128)S(1)} fusion(f32[8,512,128]{2,1,0:T(8,128)} %param.6, f32[8,512,128]{2,1,0:T(8,128)} %param.7, s32[8,512,128]{2,1,0:T(8,128)} %param.8), kind=kLoop, calls=%fused_computation.8 | loop fusion | flops 1572864 | bytes 8388608 | tf_op jit(solution)/shard_map/mul | solution.py:147
  4.2 3.4 %fusion.14 = f32[8,4,128,128]{2,3,1,0:T(8,128)} fusion(f32[8,4,128,128]{3,2,1,0:T(8,128)S(1)} %bitcast.310, f32[128,128]{1,0:T(8,128)S(1)} %get-tuple-element.62, f32[128,128]{1,0:T(8,128)S(1)} %get-tuple-element.60, f32[128,128]{1,0:T(8,128)S(1)} %get-tuple-element.61, f32[128,128]{1,0:T(8,128)S(1)} %get-tuple-element.59, f32[8]{0:T(128)S(1)} %get-tuple-element.58, ...), kind=kOutput, calls=%fused_computation.47 | convolution fusion | flops 806223872 | bytes 4472896 | tf_op jit(solution)/shard_map/lpq,lbqw->lbpw/dot_general | solution.py:107
  15.6 6.4 %all-gather = f32[32,1,4,128]{3,2,1,0:T(4,128)S(1)} all-gather(f32[8,1,4,128]{3,2,1,0:T(4,128)S(1)} %bitcast.326), channel_id=2, replica_groups=mesh['gx'=4,'gy'=8] {'gx'}, dimensions={0}, use_global_device_ids=true | all-gather | bytes 81920 | tf_op jit(solution)/shard_map/all_gather | solution.py:92
  23.7 2.2 convolution_add_fusion.3
  25.9 1.6 bitcast_multiply_fusion.3
  29.5 4.9 %fusion.10 = f32[8,4,128,128]{2,3,1,0:T(8,128)} fusion(f32[8,4,128,128]{3,2,1,0:T(8,128)} %bitcast.314, f32[8,128,128]{2,1,0:T(8,128)S(1)} %rev.24), kind=kOutput, calls=%fused_computation.43 | convolution fusion | flops 805306368 | bytes 4718592 | tf_op jit(solution)/shard_map/lpq,lbqw->lbpw/dot_general | solution.py:107
  35.3 2.8 %fusion.127 = f32[8,4,128,4]{2,3,1,0:T(4,128)S(1)} fusion(f32[8,4,128,128]{3,2,1,0:T(8,128)} %bitcast.315, f32[8,4,128]{2,1,0:T(4,128)S(1)} %rev.25), kind=kOutput, calls=%fused_computation.176 | convolution fusion | flops 25165824 | bytes 2179072 | tf_op jit(solution)/shard_map/lkq,lbqw->lbkw/dot_general | solution.py:108
  38.9 5.8 %all-gather.1 = f32[32,1,4,128]{3,2,1,0:T(4,128)S(1)} all-gather(f32[8,1,4,128]{3,2,1,0:T(4,128)S(1)} %bitcast.327), channel_id=3, replica_groups=mesh['gx'=4,'gy'=8] {'gx'}, dimensions={0}, use_global_device_ids=true | all-gather | bytes 81920 | tf_op jit(solution)/shard_map/all_gather | solution.py:92
  46.3 3.5 %convolution_add_fusion.2 = f32[8,4,128,128]{2,3,1,0:T(8,128)S(1)} fusion(f32[8,4,128,128]{2,3,1,0:T(8,128)} %fusion.10, f32[8,4,4,128]{3,1,2,0:T(4,128)S(1)} %convolution_add_fusion.6, f32[8,128,4]{1,2,0:T(4,128)S(1)} %rev.26), kind=kOutput, calls=%fused_computation.11 | convolution fusion | flops 25690112 | bytes 4276224 | tf_op jit(solution)/shard_map/lpk,lbkw->lbpw/dot_general | solution.py:139
  51.5 3.4 %fusion.211 = f32[8,512,128]{2,1,0:T(8,128)} fusion(f32[8,512,128]{2,1,0:T(8,128)S(1)} %bitcast_multiply_fusion.2, f32[8]{0:T(128)S(1)} %copy-done.74, f32[8]{0:T(128)S(1)} %copy-done.97, f32[128,128]{1,0:T(8,128)S(1)} %get-tuple-element.62, f32[128,128]{1,0:T(8,128)S(1)} %get-tuple-element.60, f32[128,128]{1,0:T(8,128)S(1)} %get-tuple-element.61, ...), kind=kOutput, calls=%fused_computation.370 | convolution fusion | flops 806223872 | bytes 4472896 | tf_op jit(solution)/shard_map/lpq,lwbq->lwbp/dot_general | solution.py:112
  56.4 3.6 %convolution_bitcast_fusion.15 = f32[8,4,512,1]{2,1,3,0:T(4,128)S(1)} fusion(f32[8,512,128]{2,1,0:T(8,128)} %copy-done.2, f32[8,128]{1,0:T(8,128)S(1)} %copy-done.37, f32[8,4]{1,0:T(8,128)S(1)} %copy-done.28, f32[4,128]{1,0:T(4,128)S(1)} %copy-done.23), kind=kOutput, calls=%fused_computation.30 | convolution fusion | flops 25174016 | bytes 2168960 | tf_op jit(solution)/shard_map/lkq,lwbq->lbkw/dot_general | solution.py:113
  61.8 32.6 %all-gather.2 = f32[64,1,4,512]{3,2,1,0:T(4,128)S(1)} all-gather(f32[8,1,4,512]{3,2,1,0:T(4,128)S(1)} %slice.86), channel_id=4, replica_groups=mesh['gx'=4,'gy'=8] {'gy'}, dimensions={0}, use_global_device_ids=true | all-gather | bytes 589824 | tf_op jit(solution)/shard_map/all_gather | solution.py:95
  95.8 4.9 %add_multiply_fusion.1 = f32[8,512,128]{2,1,0:T(8,128)} fusion(f32[8,512,128]{2,1,0:T(8,128)S(1)} %copy-done.3, s32[8,512,128]{2,1,0:T(8,128)S(1)} %copy-done, f32[8,4,512]{2,1,0:T(4,128)S(1)} %fusion.1, f32[8,1,4]{2,0,1:T(8,128)S(1)} %copy.116, f32[8,128]{1,0:T(8,128)S(1)} %copy-done.35, f32[128,1,4]{0,2,1:T(4,128)S(1)} %copy-done.26, ...), kind=kOutput, calls=%fused_computation.7 | convolution fusion | flops 26750976 | bytes 6363268 | tf_op jit(solution)/shard_map/lpk,lbkw->lwbp/dot_general | solution.py:141
  100.8 3.8 %rev.27 = f32[8,128,128]{2,1,0:T(8,128)S(1)} reverse(f32[8,128,128]{2,1,0:T(8,128)} %get-tuple-element.10), dimensions={1,2} | reverse | bytes 1048576 | tf_op jit(solution)/shard_map/rev | solution.py:73
  104.6 4.8 %fusion.212 = f32[8,512,128]{2,1,0:T(8,128)} fusion(f32[8,512,128]{2,1,0:T(8,128)} %add_multiply_fusion.1, f32[8,128,128]{2,1,0:T(8,128)S(1)} %rev.27), kind=kOutput, calls=%fused_computation.371 | convolution fusion | flops 805306368 | bytes 4718592 | tf_op jit(solution)/shard_map/lpq,lwbq->lwbp/dot_general | solution.py:112
  111.4 3.4 %convolution_bitcast_fusion.12 = f32[8,4,512,1]{2,1,3,0:T(4,128)S(1)} fusion(f32[8,512,128]{2,1,0:T(8,128)} %add_multiply_fusion.1, f32[8,4,128]{2,1,0:T(4,128)} %rev.28), kind=kOutput, calls=%fused_computation.27 | convolution fusion | flops 25165824 | bytes 2179072 | tf_op jit(solution)/shard_map/lkq,lwbq->lbkw/dot_general | solution.py:113
  115.8 31.4 %all-gather.3 = f32[64,1,4,512]{3,2,1,0:T(4,128)S(1)} all-gather(f32[8,1,4,512]{3,2,1,0:T(4,128)S(1)} %slice.91), channel_id=5, replica_groups=mesh['gx'=4,'gy'=8] {'gy'}, dimensions={0}, use_global_device_ids=true | all-gather | bytes 589824 | tf_op jit(solution)/shard_map/all_gather | solution.py:95
  151.3 6.0 %multiply_select_fusion = f32[8,512,128]{2,1,0:T(8,128)S(1)} fusion(f32[8,512,128]{2,1,0:T(8,128)} %copy-done.1, f32[8,512,128]{2,1,0:T(8,128)} %fusion.212, s32[8,512,128]{2,1,0:T(8,128)S(1)} %copy-done, f32[8,4,512]{2,1,0:T(4,128)} %fusion.3, f32[8,128,4]{1,2,0:T(4,128)} %rev.29, pred[8]{0:T(512)(128)(4,1)S(1)} %get-tuple-element.33), kind=kOutput, calls=%fused_computation.6 | convolution fusion | flops 27262976 | bytes 8470536 | tf_op jit(solution)/shard_map/lpk,lbkw->lwbp/dot_general | solution.py:141
  157.4 2.1 fusion.12
  161.7 5.4 %all-gather.4 = f32[32,1,4,128]{3,2,1,0:T(4,128)S(1)} all-gather(f32[8,1,4,128]{3,2,1,0:T(4,128)S(1)} %bitcast.328), channel_id=6, replica_groups=mesh['gx'=4,'gy'=8] {'gx'}, dimensions={0}, use_global_device_ids=true | all-gather | bytes 81920 | tf_op jit(solution)/shard_map/all_gather | solution.py:92
  167.9 2.1 convolution_add_fusion.1
  170.3 2.0 fusion.8
  174.4 5.5 %all-gather.5 = f32[32,1,4,128]{3,2,1,0:T(4,128)S(1)} all-gather(f32[8,1,4,128]{3,2,1,0:T(4,128)S(1)} %bitcast.329), channel_id=7, replica_groups=mesh['gx'=4,'gy'=8] {'gx'}, dimensions={0}, use_global_device_ids=true | all-gather | bytes 81920 | tf_op jit(solution)/shard_map/all_gather | solution.py:92
  180.6 1.9 convolution_add_fusion
  183.1 2.1 fusion.210
  185.4 1.9 convolution_bitcast_fusion.9
  187.7 31.8 %all-gather.6 = f32[64,1,4,512]{3,2,1,0:T(4,128)S(1)} all-gather(f32[8,1,4,512]{3,2,1,0:T(4,128)S(1)} %slice.97), channel_id=8, replica_groups=mesh['gx'=4,'gy'=8] {'gy'}, dimensions={0}, use_global_device_ids=true | all-gather | bytes 589824 | tf_op jit(solution)/shard_map/all_gather | solution.py:95
  220.9 3.6 %add_multiply_fusion = f32[8,512,128]{2,1,0:T(8,128)S(1)} fusion(f32[8,512,128]{2,1,0:T(8,128)S(1)} %fusion.210, s32[8,512,128]{2,1,0:T(8,128)S(1)} %copy-done, f32[8,4,512]{2,1,0:T(4,128)S(1)} %fusion.5, f32[8,1,4]{2,0,1:T(8,128)S(1)} %copy-done.31, f32[8,128]{1,0:T(8,128)S(1)} %copy-done.36, f32[128,1,4]{0,2,1:T(4,128)S(1)} %copy-done.27, ...), kind=kOutput, calls=%fused_computation.5 | convolution fusion | flops 26750976 | bytes 6363268 | tf_op jit(solution)/shard_map/lpk,lbkw->lwbp/dot_general | solution.py:141
  224.5 1.9 fusion.213
  226.6 1.9 convolution_bitcast_fusion.6
  228.8 31.5 %all-gather.7 = f32[64,1,4,512]{3,2,1,0:T(4,128)S(1)} all-gather(f32[8,1,4,512]{3,2,1,0:T(4,128)S(1)} %slice.99), channel_id=9, replica_groups=mesh['gx'=4,'gy'=8] {'gy'}, dimensions={0}, use_global_device_ids=true | all-gather | bytes 589824 | tf_op jit(solution)/shard_map/all_gather | solution.py:95
  261.8 5.4 %select_multiply_fusion = f32[8,512,128]{2,1,0:T(8,128)} fusion(f32[8,512,128]{2,1,0:T(8,128)S(1)} %copy-done.5, f32[8,512,128]{2,1,0:T(8,128)S(1)} %multiply_select_fusion, f32[8,512,128]{2,1,0:T(8,128)S(1)} %fusion.213, s32[8,512,128]{2,1,0:T(8,128)S(1)} %copy-done, f32[8,4,512]{2,1,0:T(4,128)S(1)} %fusion.7, f32[8,128,4]{1,2,0:T(4,128)S(1)} %copy-done.13, ...), kind=kOutput, calls=%fused_computation.4 | convolution fusion | flops 27787264 | bytes 10567688 | tf_op jit(solution)/shard_map/lpk,lbkw->lwbp/dot_general | solution.py:141
  (371 shorter events, 38.5 us)
Async XLA Ops:
  45.4 50.4 %copy-start.30 = (f32[8,1,4]{2,0,1:T(8,128)}, f32[8,1,4]{2,0,1:T(8,128)S(1)}, u32[]{:S(2)}) copy-start(f32[8,1,4]{2,0,1:T(8,128)S(1)} %copy.116) | copy-start | bytes 388
  55.0 40.4 %copy-start.19 = (f32[4,4]{1,0:T(4,128)S(1)}, f32[4,4]{1,0:T(4,128)}, u32[]{:S(2)}) copy-start(f32[4,4]{1,0:T(4,128)} %copy-done.18) | copy-start | bytes 196
  55.0 40.5 %copy-start.68 = (f32[8]{0:T(128)S(1)}, f32[8]{0:T(128)}, u32[]{:S(2)}) copy-start(f32[8]{0:T(128)} %copy-done.67) | copy-start | bytes 100
  55.0 40.5 %copy-start.87 = (f32[8]{0:T(128)S(1)}, f32[8]{0:T(128)}, u32[]{:S(2)}) copy-start(f32[8]{0:T(128)} %get-tuple-element.42) | copy-start | bytes 100
  55.8 40.1 %copy-start.82 = (f32[8,4,4]{2,1,0:T(4,128)}, f32[8,4,4]{2,1,0:T(4,128)S(1)}, u32[]{:S(2)}) copy-start(f32[8,4,4]{2,1,0:T(4,128)S(1)} %get-tuple-element.21) | copy-start | bytes 1540
  56.4 39.4 %copy-start.111 = (f32[8,8]{1,0:T(8,128)}, f32[8,8]{1,0:T(8,128)S(1)}, u32[]{:S(2)}) copy-start(f32[8,8]{1,0:T(8,128)S(1)} %get-tuple-element.35) | copy-start | bytes 772
  56.4 39.4 %copy-start.128 = (pred[8]{0:T(512)(128)(4,1)}, pred[8]{0:T(512)(128)(4,1)S(1)}, u32[]{:S(2)}) copy-start(pred[8]{0:T(512)(128)(4,1)S(1)} %fusion.188) | copy-start | bytes 28
  56.4 39.4 %copy-start.3 = (f32[8,512,128]{2,1,0:T(8,128)S(1)}, f32[8,512,128]{2,1,0:T(8,128)}, u32[]{:S(2)}) copy-start(f32[8,512,128]{2,1,0:T(8,128)} %fusion.211) | copy-start | bytes 6291460
  60.7 40.0 %copy-start.57 = (f32[2,4,4]{2,1,0:T(4,128)}, f32[2,4,4]{2,1,0:T(4,128)S(1)}, u32[]{:S(2)}) copy-start(f32[2,4,4]{2,1,0:T(4,128)S(1)} %get-tuple-element.23) | copy-start | bytes 388
  61.4 39.3 %copy-start.61 = (f32[8,2]{1,0:T(8,128)}, f32[8,2]{1,0:T(8,128)S(1)}, u32[]{:S(2)}) copy-start(f32[8,2]{1,0:T(8,128)S(1)} %get-tuple-element.37) | copy-start | bytes 196
  61.4 39.3 %copy-start.113 = (pred[2]{0:T(512)(128)(4,1)}, pred[2]{0:T(512)(128)(4,1)S(1)}, u32[]{:S(2)}) copy-start(pred[2]{0:T(512)(128)(4,1)S(1)} %fusion.189) | copy-start | bytes 10
  111.3 35.9 %copy-start.80 = (f32[8,4,4]{2,1,0:T(4,128)S(1)}, f32[8,4,4]{2,1,0:T(4,128)}, u32[]{:S(2)}) copy-start(f32[8,4,4]{2,1,0:T(4,128)} %get-tuple-element.20) | copy-start | bytes 1540
  111.3 35.8 %copy-start.109 = (f32[8,8]{1,0:T(8,128)S(1)}, f32[8,8]{1,0:T(8,128)}, u32[]{:S(2)}) copy-start(f32[8,8]{1,0:T(8,128)} %get-tuple-element.34) | copy-start | bytes 772
  111.3 35.8 %copy-start.130 = (pred[8]{0:T(512)(128)(4,1)S(1)}, pred[8]{0:T(512)(128)(4,1)}, u32[]{:S(2)}) copy-start(pred[8]{0:T(512)(128)(4,1)} %fusion.191) | copy-start | bytes 28
  111.3 36.9 %copy-start.20 = (f32[4,4]{1,0:T(4,128)S(1)}, f32[4,4]{1,0:T(4,128)}, u32[]{:S(2)}) copy-start(f32[4,4]{1,0:T(4,128)} %copy-done.18) | copy-start | bytes 196
  111.3 36.9 %copy-start.49 = (f32[4,4]{1,0:T(4,128)S(1)}, f32[4,4]{1,0:T(4,128)}, u32[]{:S(2)}) copy-start(f32[4,4]{1,0:T(4,128)} %copy-done.48) | copy-start | bytes 196
  111.4 36.9 %copy-start.69 = (f32[8]{0:T(128)S(1)}, f32[8]{0:T(128)}, u32[]{:S(2)}) copy-start(f32[8]{0:T(128)} %copy-done.67) | copy-start | bytes 100
  111.4 36.9 %copy-start.88 = (f32[8]{0:T(128)S(1)}, f32[8]{0:T(128)}, u32[]{:S(2)}) copy-start(f32[8]{0:T(128)} %get-tuple-element.42) | copy-start | bytes 100
  185.3 34.1 %copy-start.83 = (f32[8,4,4]{2,1,0:T(4,128)S(1)}, f32[8,4,4]{2,1,0:T(4,128)}, u32[]{:S(2)}) copy-start(f32[8,4,4]{2,1,0:T(4,128)} %copy-done.82) | copy-start | bytes 1540
  185.3 34.1 %copy-start.112 = (f32[8,8]{1,0:T(8,128)S(1)}, f32[8,8]{1,0:T(8,128)}, u32[]{:S(2)}) copy-start(f32[8,8]{1,0:T(8,128)} %copy-done.111) | copy-start | bytes 772
  185.4 34.1 %copy-start.129 = (pred[8]{0:T(512)(128)(4,1)S(1)}, pred[8]{0:T(512)(128)(4,1)}, u32[]{:S(2)}) copy-start(pred[8]{0:T(512)(128)(4,1)} %copy-done.128) | copy-start | bytes 28
  185.4 35.2 %copy-start.21 = (f32[4,4]{1,0:T(4,128)S(1)}, f32[4,4]{1,0:T(4,128)}, u32[]{:S(2)}) copy-start(f32[4,4]{1,0:T(4,128)} %copy-done.18) | copy-start | bytes 196
  185.4 35.1 %copy-start.50 = (f32[4,4]{1,0:T(4,128)S(1)}, f32[4,4]{1,0:T(4,128)}, u32[]{:S(2)}) copy-start(f32[4,4]{1,0:T(4,128)} %copy-done.48) | copy-start | bytes 196
  185.4 35.1 %copy-start.70 = (f32[8]{0:T(128)S(1)}, f32[8]{0:T(128)}, u32[]{:S(2)}) copy-start(f32[8]{0:T(128)} %copy-done.67) | copy-start | bytes 100
  185.4 35.1 %copy-start.89 = (f32[8]{0:T(128)S(1)}, f32[8]{0:T(128)}, u32[]{:S(2)}) copy-start(f32[8]{0:T(128)} %get-tuple-element.42) | copy-start | bytes 100
  185.4 35.5 %copy-start.31 = (f32[8,1,4]{2,0,1:T(8,128)S(1)}, f32[8,1,4]{2,0,1:T(8,128)}, u32[]{:S(2)}) copy-start(f32[8,1,4]{2,0,1:T(8,128)} %copy-done.30) | copy-start | bytes 388
  185.4 35.5 %copy-start.36 = (f32[8,128]{1,0:T(8,128)S(1)}, f32[8,128]{1,0:T(8,128)}, u32[]{:S(2)}) copy-start(f32[8,128]{1,0:T(8,128)} %get-tuple-element.38) | copy-start | bytes 12292
  226.5 33.8 %copy-start.81 = (f32[8,4,4]{2,1,0:T(4,128)S(1)}, f32[8,4,4]{2,1,0:T(4,128)}, u32[]{:S(2)}) copy-start(f32[8,4,4]{2,1,0:T(4,128)} %get-tuple-element.20) | copy-start | bytes 1540
  226.5 33.8 %copy-start.110 = (f32[8,8]{1,0:T(8,128)S(1)}, f32[8,8]{1,0:T(8,128)}, u32[]{:S(2)}) copy-start(f32[8,8]{1,0:T(8,128)} %get-tuple-element.34) | copy-start | bytes 772
  226.5 33.8 %copy-start.131 = (pred[8]{0:T(512)(128)(4,1)S(1)}, pred[8]{0:T(512)(128)(4,1)}, u32[]{:S(2)}) copy-start(pred[8]{0:T(512)(128)(4,1)} %fusion.191) | copy-start | bytes 28
  226.5 35.2 %copy-start.5 = (f32[8,512,128]{2,1,0:T(8,128)S(1)}, f32[8,512,128]{2,1,0:T(8,128)}, u32[]{:S(2)}) copy-start(f32[8,512,128]{2,1,0:T(8,128)} %param.7) | copy-start | bytes 6291460
  226.5 35.2 %copy-start.13 = (f32[8,128,4]{1,2,0:T(4,128)S(1)}, f32[8,128,4]{1,2,0:T(4,128)}, u32[]{:S(2)}) copy-start(f32[8,128,4]{1,2,0:T(4,128)} %rev.29) | copy-start | bytes 49156
  (100 other events, 665.3 us)
where the time goes:
time: 273 us; the launch traced here: 268 us
  blocking collectives  150 us (55%)
  matrix products  84.9 us (31%)
  other arithmetic  17.7 us (6%)
  local copies, waits for them, and re-layouts  12.4 us (5%)
    all_gather x4, blocking collectives, device_carry(): pieces = lax.all_gather(device_end[None], 'gy', axis=0, tiled=True)  127 us
    all_gather x4, blocking collectives, device_carry(): pieces = lax.all_gather(device_end[None], 'gx', axis=0, tiled=True)  23.1 us
    dot_general x4, matrix products, filter_pass(): jnp.einsum('lpk,lbkw->lwbp', response, block_start, precision=highest)  19.9 us
    dot_general x4, matrix products, filter_pass(): inside = jnp.einsum('lpq,lbqw->lbpw', tile, shaped, precision=highest)  12.4 us
    dot_general x4, matrix products, filter_pass(): inside = jnp.einsum('lpq,lwbq->lwbp', tile, shaped, precision=highest)  12.4 us
    dot_general x4, matrix products, filter_pass(): closing = jnp.einsum('lkq,lwbq->lbkw', finals, shaped, precision=highest)  10.7 us
    dot_general x4, matrix products, filter_pass(): jnp.einsum('lpk,lbkw->lbpw', response, block_start, precision=highest)  9.66 us
    dot_general x4, matrix products, filter_pass(): closing = jnp.einsum('lkq,lbqw->lbkw', finals, shaped, precision=highest)  6.41 us

commit v1 on v0

v1 whole, which is shorter than its diff:
```python
import functools

import jax
import jax.numpy as jnp
from jax import lax
from jax.experimental import pallas as pl
from jax.experimental.pallas import tpu as pltpu
from jax.sharding import PartitionSpec as P

BX = 256
MAXSTEPS = 2
UNROLL = 2
gain_base = 3.0**0.125
MESH = pl.DeviceIdType.MESH
f32, bf16 = jnp.float32, jnp.bfloat16


def section_gain(decay_rate, filter_steps):
    fading = -jnp.expm1(-decay_rate)
    return gain_base * fading ** (1.0 - 1.0 / (16.0 * filter_steps.astype(f32)))


def halves(table):
    high = lax.reduce_precision(table, 8, 7)
    return high.astype(bf16), (table - high).astype(bf16)


def binomials(count):
    return (
        jnp.ones_like(count),
        count,
        count * (count + 1.0) / 2.0,
        count * (count + 1.0) * (count + 2.0) / 6.0,
    )


def powers(weight):
    return (jnp.ones_like(weight), weight, weight * weight, weight * weight * weight)


def tile_table(rate, weight, size, backward):
    places = jnp.arange(size).astype(f32)
    lagged = places[:, None] - places[None, :]
    if backward:
        lagged = -lagged
    span = jnp.maximum(lagged, 0.0)
    w = weight[:, None, None]
    return jnp.where(
        lagged > -0.5,
        (w * w * w * w) * jnp.exp(-rate[:, None, None] * span) * ((span + 1.0) * (span + 2.0) * (span + 3.0) / 6.0),
        0.0,
    )


def end_tables(rate, weight, size, backward):
    places = jnp.arange(size).astype(f32)
    if backward:
        places = size - 1.0 - places
    remain, ahead = size - places, places + 1.0
    a, w = rate[:, None], weight[:, None]
    pw = powers(w)
    fin = jnp.stack(
        [w * pw[k] * jnp.exp(-a * (remain - 1.0)) * b for k, b in enumerate(binomials(remain[None]))], 1
    )
    res = jnp.stack(
        [pw[3 - k] * jnp.exp(-a * ahead) * binomials(ahead[None])[3 - k] for k in range(4)], 1
    )
    return fin, res


def pad4(rows):
    return jnp.pad(rows, ((0, 0), (0, 4), (0, 0)))


def stacked_ends(fin, res):
    fin_hi, fin_lo = halves(pad4(fin))
    res_hi, res_lo = halves(pad4(res))
    return (
        jnp.concatenate([fin_hi, fin_lo], 1),
        jnp.concatenate([res_hi, res_hi, res_lo, jnp.zeros_like(res_lo)], 1),
    )


def step_coefs(rate, weight, spans):
    pw = powers(weight)
    out = []
    for span in spans:
        count = jnp.full_like(rate, float(span))
        fall = jnp.exp(-rate * count)
        for k, b in enumerate(binomials(count)):
            out.append(fall * pw[k] * b)
    return jnp.stack(out, 1)


def split(value):
    high = value.astype(bf16)
    return high, (value - high.astype(f32)).astype(bf16)


def kernel(
    nx, ny, levels, rows, cols,
    coef_x, coef_y, active,
    inc, dev, sea, txh, txl, fx, rx, wy, fy, ry,
    out,
    field, inside, closing_x, end_x, got_x, end_y, got_y, pass_y, chain_y, carry_y,
    sx_sem, rx_sem, sp_sem, rp_sem, sc_sem, rc_sem,
):
    gx, gy = lax.axis_index("gx"), lax.axis_index("gy")
    nb = rows // BX
    row4 = lax.broadcasted_iota(jnp.int32, (8, 128), 0) < 4
    half = ny // 2
    inner, outer = lax.rem(gy, 2), gy // 2
    partner = gy + 1 - 2 * inner

    def advance(state, coef, l, index):
        total = coef[l, 4 * index] * state
        for j in range(1, 4):
            total += coef[l, 4 * index + j] * pltpu.roll(state, j, 0)
        keep = jnp.concatenate([row4] * (state.shape[1] // 128), 1)
        return jnp.where(keep, total, 0.0)

    def three(state):
        high = state.astype(bf16).astype(f32)
        return jnp.concatenate([high, state - high, high, jnp.zeros_like(high)], 0).astype(bf16)

    def dot(a, b, ca=1, cb=0):
        return lax.dot_general(a, b, (((ca,), (cb,)), ((), ())), preferred_element_type=f32)

    def x_copy(l, stage, d, backward):
        target = gx - d if backward else gx + d
        return pltpu.make_async_remote_copy(
            src_ref=end_x.at[stage, l],
            dst_ref=got_x.at[stage, l, d - 1],
            send_sem=sx_sem.at[stage, l, d - 1],
            recv_sem=rx_sem.at[stage, l, d - 1],
            device_id=(target, gy),
            device_id_type=MESH,
        )

    def p_copy(l, stage):
        return pltpu.make_async_remote_copy(
            src_ref=end_y.at[stage, l],
            dst_ref=got_y.at[stage, l],
            send_sem=sp_sem.at[stage, l],
            recv_sem=rp_sem.at[stage, l],
            device_id=(gx, partner),
            device_id_type=MESH,
        )

    def c_copy(l, stage, backward):
        return pltpu.make_async_remote_copy(
            src_ref=pass_y.at[stage, l],
            dst_ref=chain_y.at[stage, l],
            send_sem=sc_sem.at[stage, l],
            recv_sem=rc_sem.at[stage, l],
            device_id=(gx, gy - 2 if backward else gy + 2),
            device_id_type=MESH,
        )

    def x_sends(d, backward):
        return gx >= d if backward else gx + d < nx

    def x_gets(d, backward):
        return gx + d < nx if backward else gx >= d

    def c_sends(backward):
        return outer > 0 if backward else outer < half - 1

    def c_gets(backward):
        return outer < half - 1 if backward else outer > 0

    def start_x(l, value, rep, backward):
        back = int(backward)
        stage = 2 * rep + back
        wide = jnp.concatenate([value[b * BX:(b + 1) * BX] for b in range(nb)], 1)
        high, low = split(wide)
        both = dot(fx[back, l], high) + dot(fx[back, l], low)
        closing = both[:8] + both[8:]
        closing_x[l] = closing
        order = range(nb - 1, -1, -1) if backward else range(nb)
        end = None
        for b in order:
            piece = closing[:, b * cols:(b + 1) * cols]
            end = piece if end is None else advance(end, coef_x, l, 0) + piece
        end_x[stage, l] = end
        for d in range(1, nx):
            @pl.when(x_sends(d, backward))
            def _():
                x_copy(l, stage, d, backward).start()
        th = txh[back, l]
        inside[l] = dot(th, high) + dot(th, low) + dot(txl[back, l], high)

    def fin_x(l, rep, backward):
        back = int(backward)
        stage = 2 * rep + back
        for d in range(1, nx):
            @pl.when(x_gets(d, backward))
            def _():
                x_copy(l, stage, d, backward).wait_recv()
        carry = got_x[stage, l, 0]
        for d in range(2, nx):
            carry += advance(got_x[stage, l, d - 1], coef_x, l, d - 1)
        order = list(range(nb - 1, -1, -1) if backward else range(nb))
        starts = [None] * nb
        for n, b in enumerate(order):
            starts[b] = carry
            if n < nb - 1:
                carry = advance(carry, coef_x, l, 0) + closing_x[l, :, b * cols:(b + 1) * cols]
        wide = inside[l] + dot(rx[back, l], three(jnp.concatenate(starts, 1)), 0, 0)
        value = jnp.concatenate([wide[:, b * cols:(b + 1) * cols] for b in range(nb)], 0)
        return value * sea[l].astype(f32)

    def start_y(l, value, rep, backward):
        back = int(backward)
        stage = 2 * rep + back
        high, low = split(value)
        pair = jnp.concatenate([high, low], 1)
        ends = jnp.concatenate([fy[back, l]] * 2, 1)
        both = dot(ends, pair, 1, 1)
        end_y[stage, l] = both[:8] + both[8:]
        p_copy(l, stage).start()
        wide = dot(pair, wy[back, l])
        field[l] = wide[:, :cols] + wide[:, cols:]

    def relay_y(l, rep, backward):
        back = int(backward)
        stage = 2 * rep + back
        p_copy(l, stage).wait_recv()
        own, other = end_y[stage, l], got_y[stage, l]
        is_first = inner == (1 if backward else 0)
        first = jnp.where(is_first, own, other)
        second = jnp.where(is_first, other, own)
        joint = advance(first, coef_y, l, 0) + second

        @pl.when(c_gets(backward))
        def _():
            c_copy(l, stage, backward).wait_recv()

        come = chain_y[stage, l]
        pass_y[stage, l] = advance(come, coef_y, l, 1) + joint

        @pl.when(c_sends(backward))
        def _():
            c_copy(l, stage, backward).start()

        carry_y[l] = jnp.where(is_first, come, advance(come, coef_y, l, 0) + other)

    def fin_y(l, rep, backward):
        back = int(backward)
        value = field[l] + dot(three(carry_y[l]), ry[back, l], 0, 0)
        return value * sea[l].astype(f32)

    def each(body):
        lax.fori_loop(0, levels, lambda l, c: (body(l), c)[1], 0, unroll=UNROLL)

    got_x[...] = jnp.zeros_like(got_x)
    chain_y[...] = jnp.zeros_like(chain_y)
    barrier = pltpu.get_barrier_semaphore()
    for d in range(1, nx):
        pl.semaphore_signal(barrier, inc=1, device_id=(lax.rem(gx + d, nx), gy), device_id_type=MESH)
    pl.semaphore_signal(barrier, inc=1, device_id=(gx, partner), device_id_type=MESH)

    @pl.when(outer > 0)
    def _():
        pl.semaphore_signal(barrier, inc=1, device_id=(gx, gy - 2), device_id_type=MESH)

    @pl.when(outer < half - 1)
    def _():
        pl.semaphore_signal(barrier, inc=1, device_id=(gx, gy + 2), device_id_type=MESH)

    pl.semaphore_wait(barrier, nx + jnp.minimum(outer, 1) + jnp.minimum(half - 1 - outer, 1))

    def begin(l):
        value = dev[l] * sea[l].astype(f32) * inc[l]
        out[l] = jnp.zeros_like(value)
        start_x(l, value, 0, False)

    each(begin)

    def finish(l, rep):
        value = fin_y(l, rep, True)
        share = active[l, rep]
        out[l] = share * (dev[l] * value) + (1.0 - share) * out[l]
        return value

    def repetition(rep, c):
        each(lambda l: start_x(l, fin_x(l, rep, False), rep, True))
        each(lambda l: start_y(l, fin_x(l, rep, True), rep, False))
        each(lambda l: relay_y(l, rep, False))
        each(lambda l: start_y(l, fin_y(l, rep, False), rep, True))
        each(lambda l: relay_y(l, rep, True))

        @pl.when(rep < MAXSTEPS - 1)
        def _():
            each(lambda l: start_x(l, finish(l, rep), rep + 1, False))

        @pl.when(rep == MAXSTEPS - 1)
        def _():
            each(lambda l: (finish(l, rep), None)[1])

        return c

    lax.fori_loop(0, MAXSTEPS, repetition, 0)

    def drain(l):
        for rep in range(MAXSTEPS):
            for backward in (False, True):
                stage = 2 * rep + int(backward)
                for d in range(1, nx):
                    @pl.when(x_sends(d, backward))
                    def _():
                        x_copy(l, stage, d, backward).wait_send()
                p_copy(l, stage).wait_send()

                @pl.when(c_sends(backward))
                def _():
                    c_copy(l, stage, backward).wait_send()

    lax.fori_loop(0, levels, lambda l, c: (drain(l), c)[1], 0)


def on_device(nx, ny, increment, deviation, land_sea, filter_steps, zonal_rate, meridional_rate):
    levels, rows, cols = increment.shape
    nb = rows // BX
    wx = section_gain(zonal_rate, filter_steps)
    wm = section_gain(meridional_rate, filter_steps)
    txh, txl, fx, rx, wy, fy, ry = [], [], [], [], [], [], []
    for backward in (False, True):
        high, low = halves(tile_table(zonal_rate, wx, BX, backward))
        txh.append(high)
        txl.append(low)
        fin, res = stacked_ends(*end_tables(zonal_rate, wx, BX, backward))
        fx.append(fin)
        rx.append(res)
        high, low = halves(tile_table(meridional_rate, wm, cols, not backward))
        wy.append(
            jnp.concatenate(
                [jnp.concatenate([high, low], 2), jnp.concatenate([high, jnp.zeros_like(low)], 2)], 1
            )
        )
        fin, res = stacked_ends(*end_tables(meridional_rate, wm, cols, backward))
        fy.append(fin)
        ry.append(res)
    tables = [jnp.stack(t) for t in (txh, txl, fx, rx, wy, fy, ry)]
    coef_x = step_coefs(zonal_rate, wx, [BX] + [rows * d for d in range(1, nx - 1)])
    coef_y = step_coefs(meridional_rate, wm, [cols, 2 * cols])
    active = (filter_steps[:, None] > jnp.arange(MAXSTEPS)[None]).astype(f32)
    smem = pl.BlockSpec(memory_space=pltpu.SMEM)
    vmem = pl.BlockSpec(memory_space=pltpu.VMEM)
    stages = 2 * MAXSTEPS
    dma = pltpu.SemaphoreType.DMA
    return pl.pallas_call(
        functools.partial(kernel, nx, ny, levels, rows, cols),
        out_shape=jax.ShapeDtypeStruct(increment.shape, f32),
        in_specs=[smem] * 3 + [vmem] * 10,
        out_specs=vmem,
        scratch_shapes=[
            pltpu.VMEM((levels, rows, cols), f32),
            pltpu.VMEM((levels, BX, nb * cols), f32),
            pltpu.VMEM((levels, 8, nb * cols), f32),
            pltpu.VMEM((stages, levels, 8, cols), f32),
            pltpu.VMEM((stages, levels, nx - 1, 8, cols), f32),
            pltpu.VMEM((stages, levels, 8, rows), f32),
            pltpu.VMEM((stages, levels, 8, rows), f32),
            pltpu.VMEM((stages, levels, 8, rows), f32),
            pltpu.VMEM((stages, levels, 8, rows), f32),
            pltpu.VMEM((levels, 8, rows), f32),
            dma((stages, levels, nx - 1)),
            dma((stages, levels, nx - 1)),
            dma((stages, levels)),
            dma((stages, levels)),
            dma((stages, levels)),
            dma((stages, levels)),
        ],
        compiler_params=pltpu.CompilerParams(
            collective_id=0, has_side_effects=True, vmem_limit_bytes=60 * 1024 * 1024
        ),
    )(coef_x, coef_y, active, increment, deviation, land_sea, *tables)


def solution(mesh):
    placed = (P(None, "gx", "gy"), P(None, "gx", "gy"), P(None, "gx", "gy"), P(), P(), P())
    body = functools.partial(on_device, mesh.shape["gx"], mesh.shape["gy"])
    return jax.shard_map(
        body, mesh=mesh, in_specs=placed, out_specs=P(None, "gx", "gy"), check_vma=False
    )
```

time: 273 us -> 117 us (0.43); the launches traced: 268 us -> 116 us
  blocking collectives: 150 us -> 0 us
  Pallas kernels: 0 us -> 95.9 us
  matrix products: 84.9 us -> 0 us
  local copies, waits for them, and re-layouts: 12.4 us -> 6.17 us
  other arithmetic: 17.7 us -> 14.2 us
    all_gather x8 -> x0, blocking collectives: 150 us -> none  [the longest x4 127 us: device_carry(): pieces = lax.all_gather(device_end[None], 'gy', axis=0, tiled=True)]
    pallas_call x0 -> x1, Pallas kernels: none -> 95.9 us  [on_device(): pl.pallas_call(functools.partial(kernel, nx, ny, levels, rows, cols), out...]
    dot_general x48 -> x0, matrix products: 84.9 us -> none  [the longest x4 19.9 us: filter_pass(): jnp.einsum('lpk,lbkw->lwbp', response, block_start, precision=highest)]
    another operation x0 -> x17, other arithmetic: none -> 9 us  [the longest x15 7.63 us: on_device(): tables = [jnp.stack(t) for t in (txh, txl, fx, rx, wy, fy, ry)]]
    rev x6 -> x0, local copies, waits for them, and re-layouts: 7.51 us -> none  [the longest x2 4.48 us: block_tables(): tile = tile[:, ::-1, ::-1]]
    mul x8 -> x3, other arithmetic: 7.06 us -> 1 us  [the longest x1 0.7 us: powers(): weight * weight]
    select_n x9 -> x0, other arithmetic: 4.28 us -> none  [the longest x6 2.89 us: transfer(): jnp.where(offset < 0.5, 1.0, jnp.where(offset < 1.5, count, jnp.where(off...]
    convert_element_type x6 -> x13, other arithmetic: 0.11 us -> 3.55 us  [the longest x10 2.25 us: halves(): return (high.astype(bf16), (table - high).astype(bf16))]
where the time goes in v1:
time: 117 us; the launch traced here: 116 us
  Pallas kernels  95.9 us (82%)
  other arithmetic  14.2 us (12%)
  local copies, waits for them, and re-layouts  6.17 us (5%)
    pallas_call x1, Pallas kernels, on_device(): pl.pallas_call(functools.partial(kernel, nx, ny, levels, rows, cols), out...  95.9 us
    another operation x15, other arithmetic, on_device(): tables = [jnp.stack(t) for t in (txh, txl, fx, rx, wy, fy, ry)]  7.63 us
    unnamed x1, local copies, waits for them, and re-layouts  3.06 us
    another operation x22, local copies, waits for them, and re-layouts, step_coefs(): return jnp.stack(out, 1)  2.96 us

profile of v1, /device:TPU:0, one launch (start us, length us, event | category | flops | bytes accessed | tf_op | source)
XLA Modules:
  0.0 116.5 jit_solution(558884923327485027)
XLA Ops:
  0.2 0.7 fusion.48
  1.0 1.3 %fusion.34.active = f32[8,2]{1,0:T(8,128)} fusion(s32[8]{0:T(128)} %param.9), kind=kLoop, calls=%fused_computation.145 | loop fusion | flops 32 | bytes 96 | tf_op jit(solution)/shard_map/convert_element_type | solution.py:347
  2.3 0.7 multiply_bitcast_fusion
  3.0 0.1 copy.46
  3.2 0.1 copy.45
  3.3 0.1 copy.42
  3.6 0.1 copy.43
  3.7 0.7 stack.198.coef_y
  4.3 0.7 multiply_bitcast_fusion.6
  5.0 0.1 copy.38
  6.0 0.7 stack.189.coef_x
  6.6 0.1 fusion.19
  6.7 0.1 multiply_multiply_fusion.17
  7.1 0.6 pad_maximum_fusion.6.fy
  7.7 0.1 maximum_bitcast_fusion.4
  7.8 0.7 pad_maximum_fusion.5.ry
  8.5 0.2 broadcast_multiply_fusion
  8.9 0.7 pad_maximum_fusion.4.fx
  9.6 0.1 maximum_bitcast_fusion
  9.7 0.7 pad_maximum_fusion.3.rx
  10.4 0.2 subtract_compare_fusion
  10.6 0.1 fusion.18
  10.7 0.5 fusion.8
  11.1 0.1 fusion.5
  11.2 0.2 subtract_maximum_fusion
  11.5 0.1 fusion.7
  11.6 1.5 %pad_maximum_fusion.2.wy = bf16[2,8,256,256]{3,2,1,0:T(8,128)(2,1)} fusion(bf16[1,8,256,256]{3,2,1,0:T(8,128)(2,1)S(1)} %fusion.7, bf16[1,8,256,256]{3,2,1,0:T(8,128)(2,1)S(1)} %fusion.5), kind=kLoop, calls=%fused_computation.11 | loop fusion | flops 1048576 | bytes 4194304 | tf_op jit(solution)/shard_map/stack | solution.py:344
  13.0 1.4 %fusion = (bf16[1,8,256,256]{3,2,1,0:T(8,128)(2,1)S(1)}, bf16[1,8,256,256]{3,2,1,0:T(8,128)(2,1)S(1)}, bf16[1,8,256,256]{3,2,1,0:T(8,128)(2,1)S(1)}, bf16[1,8,256,256]{3,2,1,0:T(8,128)(2,1)S(1)}) fusion(f32[256,256]{1,0:T(8,128)S(1)} %get-tuple-element.92, f32[256,256]{1,0:T(8,128)S(1)} %get-tuple-element.91, f32[8]{0:T(128)S(1)} %get-tuple-element.126, ...), kind=kLoop, calls=%fused_computation.4 | loop fusion | flops 8388608 | bytes 5374016 | tf_op jit(solution)/shard_map/convert_element_type | solution.py:25
  14.5 1.5 %pad_maximum_fusion.1.txl = bf16[2,8,256,256]{3,2,1,0:T(8,128)(2,1)} fusion(bf16[1,8,256,256]{3,2,1,0:T(8,128)(2,1)S(1)} %get-tuple-element.88, bf16[1,8,256,256]{3,2,1,0:T(8,128)(2,1)S(1)} %get-tuple-element.10), kind=kLoop, calls=%fused_computation.10 | loop fusion | flops 1048576 | bytes 4194304 | tf_op jit(solution)/shard_map/stack | solution.py:344
  16.0 1.5 %pad_maximum_fusion.txh = bf16[2,8,256,256]{3,2,1,0:T(8,128)(2,1)} fusion(bf16[1,8,256,256]{3,2,1,0:T(8,128)(2,1)S(1)} %get-tuple-element.87, bf16[1,8,256,256]{3,2,1,0:T(8,128)(2,1)S(1)} %get-tuple-element.11), kind=kLoop, calls=%fused_computation.9 | loop fusion | flops 1048576 | bytes 4194304 | tf_op jit(solution)/shard_map/stack | solution.py:344
  17.5 95.9 %shard_map.64 = f32[8,512,128]{2,1,0:T(8,128)} custom-call(f32[8,12]{1,0:T(8,128)} %stack.189.coef_x, f32[8,8]{1,0:T(8,128)} %stack.198.coef_y, f32[8,2]{1,0:T(8,128)} %fusion.34.active, f32[8,512,128]{2,1,0:T(8,128)} %inc.1, f32[8,512,128]{2,1,0:T(8,128)} %dev.1, s32[8,512,128]{2,1,0:T(8,128)} %sea.1, bf16[2,8,256,256]{3,2,1,0:T(8,128)(2,1)} %pad_maximum_fusion.txh, ...), custom_call_target="tpu_custom_call" | custom-call | tf_op jit(solution)/shard_map/pallas_call | solution.py:352
  113.4 3.1 %copy.62 = f32[8,512,128]{2,1,0:T(8,128)} copy(f32[8,512,128]{2,1,0:T(8,128)} %shard_map.64) | data formatting | bytes 4194304
  (44 shorter events, 1.8 us)

commit v2 on v1

--- a/solution.py
+++ b/solution.py
@@ -18,11 +18,6 @@
 def section_gain(decay_rate, filter_steps):
     fading = -jnp.expm1(-decay_rate)
     return gain_base * fading ** (1.0 - 1.0 / (16.0 * filter_steps.astype(f32)))
-
-
-def halves(table):
-    high = lax.reduce_precision(table, 8, 7)
-    return high.astype(bf16), (table - high).astype(bf16)
 
 
 def binomials(count):
@@ -34,62 +29,11 @@
     )
 
 
-def powers(weight):
-    return (jnp.ones_like(weight), weight, weight * weight, weight * weight * weight)
-
-
-def tile_table(rate, weight, size, backward):
-    places = jnp.arange(size).astype(f32)
-    lagged = places[:, None] - places[None, :]
-    if backward:
-        lagged = -lagged
-    span = jnp.maximum(lagged, 0.0)
-    w = weight[:, None, None]
-    return jnp.where(
-        lagged > -0.5,
-        (w * w * w * w) * jnp.exp(-rate[:, None, None] * span) * ((span + 1.0) * (span + 2.0) * (span + 3.0) / 6.0),
-        0.0,
-    )
-
-
-def end_tables(rate, weight, size, backward):
-    places = jnp.arange(size).astype(f32)
-    if backward:
-        places = size - 1.0 - places
-    remain, ahead = size - places, places + 1.0
-    a, w = rate[:, None], weight[:, None]
-    pw = powers(w)
-    fin = jnp.stack(
-        [w * pw[k] * jnp.exp(-a * (remain - 1.0)) * b for k, b in enumerate(binomials(remain[None]))], 1
-    )
-    res = jnp.stack(
-        [pw[3 - k] * jnp.exp(-a * ahead) * binomials(ahead[None])[3 - k] for k in range(4)], 1
-    )
-    return fin, res
-
-
-def pad4(rows):
-    return jnp.pad(rows, ((0, 0), (0, 4), (0, 0)))
-
-
-def stacked_ends(fin, res):
-    fin_hi, fin_lo = halves(pad4(fin))
-    res_hi, res_lo = halves(pad4(res))
-    return (
-        jnp.concatenate([fin_hi, fin_lo], 1),
-        jnp.concatenate([res_hi, res_hi, res_lo, jnp.zeros_like(res_lo)], 1),
-    )
-
-
-def step_coefs(rate, weight, spans):
-    pw = powers(weight)
-    out = []
-    for span in spans:
-        count = jnp.full_like(rate, float(span))
-        fall = jnp.exp(-rate * count)
-        for k, b in enumerate(binomials(count)):
-            out.append(fall * pw[k] * b)
-    return jnp.stack(out, 1)
+def by_row(values, row):
+    total = jnp.zeros(row.shape, f32)
+    for k, value in enumerate(values):
+        total = jnp.where(row == k, value, total)
+    return total
 
 
 def split(value):
@@ -99,25 +43,27 @@
 
 def kernel(
     nx, ny, levels, rows, cols,
-    coef_x, coef_y, active,
-    inc, dev, sea, txh, txl, fx, rx, wy, fy, ry,
+    steps, rate_x, rate_y, gains,
+    inc, dev, sea,
     out,
+    txh, txl, fx, rx, wy, fy, ry, coef_x, coef_y,
     field, inside, closing_x, end_x, got_x, end_y, got_y, pass_y, chain_y, carry_y,
     sx_sem, rx_sem, sp_sem, rp_sem, sc_sem, rc_sem,
 ):
     gx, gy = lax.axis_index("gx"), lax.axis_index("gy")
     nb = rows // BX
-    row4 = lax.broadcasted_iota(jnp.int32, (8, 128), 0) < 4
     half = ny // 2
     inner, outer = lax.rem(gy, 2), gy // 2
     partner = gy + 1 - 2 * inner
 
     def advance(state, coef, l, index):
-        total = coef[l, 4 * index] * state
-        for j in range(1, 4):
-            total += coef[l, 4 * index + j] * pltpu.roll(state, j, 0)
-        keep = jnp.concatenate([row4] * (state.shape[1] // 128), 1)
-        return jnp.where(keep, total, 0.0)
+        copies = state.shape[1] // 128
+        total = None
+        for j in range(4):
+            scale = jnp.concatenate([coef[l, 4 * index + j]] * copies, 1)
+            term = scale * (pltpu.roll(state, j, 0) if j else state)
+            total = term if total is None else total + term
+        return total
 
     def three(state):
         high = state.astype(bf16).astype(f32)
@@ -253,6 +199,72 @@
     def each(body):
         lax.fori_loop(0, levels, lambda l, c: (body(l), c)[1], 0, unroll=UNROLL)
 
+    side = 128
+    lags = (
+        lax.broadcasted_iota(jnp.int32, (side, side), 0) - lax.broadcasted_iota(jnp.int32, (side, side), 1)
+    ).astype(f32)
+
+    def shape_of(lag):
+        span = jnp.maximum(lag, 0.0)
+        return span, jnp.where(lag > -0.5, (span + 1.0) * (span + 2.0) * (span + 3.0) / 6.0, 0.0)
+
+    near = (shape_of(lags), shape_of(-lags))
+    far = (shape_of(side + lags), shape_of(side - lags))
+
+    def tile(shape, rate, weight4):
+        return split(weight4 * shape[1] * jnp.exp(-rate * shape[0]))
+
+    def ends(fin, res, l, size, rate, weight):
+        row = lax.broadcasted_iota(jnp.int32, (8, size), 0)
+        lane = lax.broadcasted_iota(jnp.int32, (8, size), 1).astype(f32)
+        pw = [jnp.full((8, size), v) for v in (1.0, weight, weight * weight, weight * weight * weight)]
+        for back in (0, 1):
+            places = size - 1.0 - lane if back else lane
+            remain, ahead = size - places, places + 1.0
+            leave, come = binomials(remain), binomials(ahead)
+            final = by_row([weight * pw[k] * leave[k] for k in range(4)], row) * jnp.exp(-rate * (remain - 1.0))
+            high = final.astype(bf16).astype(f32)
+            fin[back, l] = jnp.concatenate([high, final - high], 0).astype(bf16)
+            answer = by_row([pw[3 - k] * come[3 - k] for k in range(4)], row) * jnp.exp(-rate * ahead)
+            high = answer.astype(bf16).astype(f32)
+            res[back, l] = jnp.concatenate(
+                [high, high, answer - high, jnp.zeros_like(high)], 0
+            ).astype(bf16)
+
+    def coefs(coef, l, spans, rate, weight):
+        row = lax.broadcasted_iota(jnp.int32, (8, 128), 0)
+        power = (1.0, weight, weight * weight, weight * weight * weight)
+        for n, span in enumerate(spans):
+            fall = jnp.where(row < 4, jnp.exp(jnp.full((8, 128), -rate * span)), 0.0)
+            count = (1.0, span, span * (span + 1.0) / 2.0, span * (span + 1.0) * (span + 2.0) / 6.0)
+            for j in range(4):
+                coef[l, 4 * n + j] = fall * (power[j] * count[j])
+
+    def build(l):
+        rate, weight = rate_x[l], gains[0, l]
+        weight4 = weight * weight * weight * weight
+        zero = jnp.zeros((side, side), bf16)
+        lower, upper = pl.ds(0, side), pl.ds(side, side)
+        for back in (0, 1):
+            one, two = tile(near[back], rate, weight4), tile(far[back], rate, weight4)
+            for ref, close, distant in ((txh, one[0], two[0]), (txl, one[1], two[1])):
+                ref[back, l, lower, lower] = close
+                ref[back, l, upper, upper] = close
+                ref[back, l, lower, upper] = distant if back else zero
+                ref[back, l, upper, lower] = zero if back else distant
+        ends(fx, rx, l, BX, rate, weight)
+        coefs(coef_x, l, [float(BX)] + [float(rows * d) for d in range(1, nx - 1)], rate, weight)
+        rate, weight = rate_y[l], gains[1, l]
+        weight4 = weight * weight * weight * weight
+        for back in (0, 1):
+            high, low = tile(near[1 - back], rate, weight4)
+            wy[back, l, lower, lower] = high
+            wy[back, l, upper, lower] = high
+            wy[back, l, lower, upper] = low
+            wy[back, l, upper, upper] = zero
+        ends(fy, ry, l, cols, rate, weight)
+        coefs(coef_y, l, [float(cols), 2.0 * cols], rate, weight)
+
     got_x[...] = jnp.zeros_like(got_x)
     chain_y[...] = jnp.zeros_like(chain_y)
     barrier = pltpu.get_barrier_semaphore()
@@ -268,6 +280,7 @@
     def _():
         pl.semaphore_signal(barrier, inc=1, device_id=(gx, gy + 2), device_id_type=MESH)
 
+    lax.fori_loop(0, levels, lambda l, c: (build(l), c)[1], 0)
     pl.semaphore_wait(barrier, nx + jnp.minimum(outer, 1) + jnp.minimum(half - 1 - outer, 1))
 
     def begin(l):
@@ -279,7 +292,7 @@
 
     def finish(l, rep):
         value = fin_y(l, rep, True)
-        share = active[l, rep]
+        share = jnp.clip((steps[l] - rep).astype(f32), 0.0, 1.0)
         out[l] = share * (dev[l] * value) + (1.0 - share) * out[l]
         return value
 
@@ -322,29 +335,7 @@
 def on_device(nx, ny, increment, deviation, land_sea, filter_steps, zonal_rate, meridional_rate):
     levels, rows, cols = increment.shape
     nb = rows // BX
-    wx = section_gain(zonal_rate, filter_steps)
-    wm = section_gain(meridional_rate, filter_steps)
-    txh, txl, fx, rx, wy, fy, ry = [], [], [], [], [], [], []
-    for backward in (False, True):
-        high, low = halves(tile_table(zonal_rate, wx, BX, backward))
-        txh.append(high)
-        txl.append(low)
-        fin, res = stacked_ends(*end_tables(zonal_rate, wx, BX, backward))
-        fx.append(fin)
-        rx.append(res)
-        high, low = halves(tile_table(meridional_rate, wm, cols, not backward))
-        wy.append(
-            jnp.concatenate(
-                [jnp.concatenate([high, low], 2), jnp.concatenate([high, jnp.zeros_like(low)], 2)], 1
-            )
-        )
-        fin, res = stacked_ends(*end_tables(meridional_rate, wm, cols, backward))
-        fy.append(fin)
-        ry.append(res)
-    tables = [jnp.stack(t) for t in (txh, txl, fx, rx, wy, fy, ry)]
-    coef_x = step_coefs(zonal_rate, wx, [BX] + [rows * d for d in range(1, nx - 1)])
-    coef_y = step_coefs(meridional_rate, wm, [cols, 2 * cols])
-    active = (filter_steps[:, None] > jnp.arange(MAXSTEPS)[None]).astype(f32)
+    gains = section_gain(jnp.stack([zonal_rate, meridional_rate]), filter_steps[None])
     smem = pl.BlockSpec(memory_space=pltpu.SMEM)
     vmem = pl.BlockSpec(memory_space=pltpu.VMEM)
     stages = 2 * MAXSTEPS
@@ -352,9 +343,18 @@
     return pl.pallas_call(
         functools.partial(kernel, nx, ny, levels, rows, cols),
         out_shape=jax.ShapeDtypeStruct(increment.shape, f32),
-        in_specs=[smem] * 3 + [vmem] * 10,
+        in_specs=[smem] * 4 + [vmem] * 3,
         out_specs=vmem,
         scratch_shapes=[
+            pltpu.VMEM((2, levels, BX, BX), bf16),
+            pltpu.VMEM((2, levels, BX, BX), bf16),
+            pltpu.VMEM((2, levels, 16, BX), bf16),
+            pltpu.VMEM((2, levels, 32, BX), bf16),
+            pltpu.VMEM((2, levels, 2 * cols, 2 * cols), bf16),
+            pltpu.VMEM((2, levels, 16, cols), bf16),
+            pltpu.VMEM((2, levels, 32, cols), bf16),
+            pltpu.VMEM((levels, 4 * (nx - 1), 8, 128), f32),
+            pltpu.VMEM((levels, 8, 8, 128), f32),
             pltpu.VMEM((levels, rows, cols), f32),
             pltpu.VMEM((levels, BX, nb * cols), f32),
             pltpu.VMEM((levels, 8, nb * cols), f32),
@@ -373,9 +373,9 @@
             dma((stages, levels)),
         ],
         compiler_params=pltpu.CompilerParams(
-            collective_id=0, has_side_effects=True, vmem_limit_bytes=60 * 1024 * 1024
+            collective_id=0, has_side_effects=True, vmem_limit_bytes=40 * 1024 * 1024
         ),
-    )(coef_x, coef_y, active, increment, deviation, land_sea, *tables)
+    )(filter_steps, zonal_rate, meridional_rate, gains, increment, deviation, land_sea)
 
 
 def solution(mesh):

time: 117 us -> 100 us (0.85)
  other arithmetic: 14.2 us -> 1.37 us
  Pallas kernels: 95.9 us -> 90.4 us
  local copies, waits for them, and re-layouts: 6.17 us -> 8.05 us
    another operation x17 -> x0, other arithmetic: 9 us -> none  [the longest x15 7.63 us: on_device(): tables = [jnp.stack(t) for t in (txh, txl, fx, rx, wy, fy, ry)]]
    pallas_call x1, Pallas kernels: 95.9 us -> 90.4 us  [on_device(): pl.pallas_call(functools.partial(kernel, nx, ny, levels, rows, cols), out...]
    unnamed x1 -> x13, local copies, waits for them, and re-layouts: 3.06 us -> 8.05 us
    convert_element_type x13 -> x0, other arithmetic: 3.55 us -> none  [the longest x10 2.25 us: halves(): return (high.astype(bf16), (table - high).astype(bf16))]
    another operation x23 -> x0, local copies, waits for them, and re-layouts: 2.96 us -> none  [the longest x22 2.96 us: step_coefs(): return jnp.stack(out, 1)]
where the time goes in v2:
time: 100 us; the launch traced here: 99.9 us
  Pallas kernels  90.4 us (90%)
  local copies, waits for them, and re-layouts  8.05 us (8%)
  other arithmetic  1.37 us (1%)
    pallas_call x1, Pallas kernels, on_device(): pl.pallas_call(functools.partial(kernel, nx, ny, levels, rows, cols), out...  90.4 us
    unnamed x13, local copies, waits for them, and re-layouts  8.05 us

profile of v2, /device:TPU:0, one launch (start us, length us, event | category | flops | bytes accessed | tf_op | source)
XLA Modules:
  0.0 99.9 jit_solution(3017848038562762753)
XLA Ops:
  0.0 0.7 divide_subtract_fusion
  0.7 0.7 fusion.3.gains
  1.4 0.0 copy-start
  1.4 1.6 %copy-done = f32[8,512,128]{2,1,0:T(8,128)S(1)} copy-done((f32[8,512,128]{2,1,0:T(8,128)S(1)}, f32[8,512,128]{2,1,0:T(8,128)}, u32[]{:S(2)}) %copy-start) | copy-done | bytes 2097176
  3.0 0.0 copy-start.1
  3.0 1.6 %copy-done.1 = f32[8,512,128]{2,1,0:T(8,128)S(1)} copy-done((f32[8,512,128]{2,1,0:T(8,128)S(1)}, f32[8,512,128]{2,1,0:T(8,128)}, u32[]{:S(2)}) %copy-start.1) | copy-done | bytes 2097176
  4.6 0.0 copy-start.2
  4.6 1.6 %copy-done.2 = s32[8,512,128]{2,1,0:T(8,128)S(1)} copy-done((s32[8,512,128]{2,1,0:T(8,128)S(1)}, s32[8,512,128]{2,1,0:T(8,128)}, u32[]{:S(2)}) %copy-start.2) | copy-done | bytes 2097176
  6.2 0.0 copy-start.3
  6.2 0.7 copy-done.3
  6.8 0.0 copy-start.4
  6.8 0.7 copy-done.4
  7.5 0.0 copy-start.5
  7.5 0.7 copy-done.5
  8.1 90.4 %shard_map.64 = f32[8,512,128]{2,1,0:T(8,128)S(1)} custom-call(s32[8]{0:T(128)S(1)} %copy-done.5, f32[8]{0:T(128)S(1)} %copy-done.3, f32[8]{0:T(128)S(1)} %copy-done.4, f32[2,8]{1,0:T(2,128)S(1)} %fusion.3.gains, f32[8,512,128]{2,1,0:T(8,128)S(1)} %copy-done, f32[8,512,128]{2,1,0:T(8,128)S(1)} %copy-done.1, s32[8,512,128]{2,1,0:T(8,128)S(1)} %copy-done.2), custom_call_target="tpu_custom_call" | custom-call | tf_op jit(solution)/shard_map/pallas_call | solution.py:343
  98.6 1.3 %copy.8 = f32[8,512,128]{2,1,0:T(8,128)} copy(f32[8,512,128]{2,1,0:T(8,128)S(1)} %shard_map.64) | data formatting | bytes 4194304
Async XLA Ops:
  1.4 1.6 %copy-start = (f32[8,512,128]{2,1,0:T(8,128)S(1)}, f32[8,512,128]{2,1,0:T(8,128)}, u32[]{:S(2)}) copy-start(f32[8,512,128]{2,1,0:T(8,128)} %inc.1) | copy-start | bytes 6291460
  3.0 1.6 %copy-start.1 = (f32[8,512,128]{2,1,0:T(8,128)S(1)}, f32[8,512,128]{2,1,0:T(8,128)}, u32[]{:S(2)}) copy-start(f32[8,512,128]{2,1,0:T(8,128)} %dev.1) | copy-start | bytes 6291460
  4.6 1.6 %copy-start.2 = (s32[8,512,128]{2,1,0:T(8,128)S(1)}, s32[8,512,128]{2,1,0:T(8,128)}, u32[]{:S(2)}) copy-start(s32[8,512,128]{2,1,0:T(8,128)} %sea.1) | copy-start | bytes 6291460
  6.2 0.7 copy-start.3
  6.8 0.7 copy-start.4
  7.5 0.7 copy-start.5

commit v3 on v2

--- a/solution.py
+++ b/solution.py
@@ -44,11 +44,11 @@
 def kernel(
     nx, ny, levels, rows, cols,
     steps, rate_x, rate_y, gains,
-    inc, dev, sea,
+    inc_hbm, dev_hbm, sea_hbm,
     out,
     txh, txl, fx, rx, wy, fy, ry, coef_x, coef_y,
-    field, inside, closing_x, end_x, got_x, end_y, got_y, pass_y, chain_y, carry_y,
-    sx_sem, rx_sem, sp_sem, rp_sem, sc_sem, rc_sem,
+    field, inside, closing_x, end_x, got_x, end_y, got_y, pass_y, chain_y, dev, sea,
+    sx_sem, rx_sem, sp_sem, rp_sem, sc_sem, rc_sem, in_sem,
 ):
     gx, gy = lax.axis_index("gx"), lax.axis_index("gy")
     nb = rows // BX
@@ -75,8 +75,8 @@
     def x_copy(l, stage, d, backward):
         target = gx - d if backward else gx + d
         return pltpu.make_async_remote_copy(
-            src_ref=end_x.at[stage, l],
-            dst_ref=got_x.at[stage, l, d - 1],
+            src_ref=end_x.at[stage, l, pl.ds(0, 4)],
+            dst_ref=got_x.at[stage, l, d - 1, pl.ds(0, 4)],
             send_sem=sx_sem.at[stage, l, d - 1],
             recv_sem=rx_sem.at[stage, l, d - 1],
             device_id=(target, gy),
@@ -85,21 +85,22 @@
 
     def p_copy(l, stage):
         return pltpu.make_async_remote_copy(
-            src_ref=end_y.at[stage, l],
-            dst_ref=got_y.at[stage, l],
+            src_ref=end_y.at[stage, l, pl.ds(0, 4)],
+            dst_ref=got_y.at[stage, l, pl.ds(0, 4)],
             send_sem=sp_sem.at[stage, l],
             recv_sem=rp_sem.at[stage, l],
             device_id=(gx, partner),
             device_id_type=MESH,
         )
 
-    def c_copy(l, stage, backward):
+    def c_copy(l, stage, d, backward):
+        target = gy - 2 * d if backward else gy + 2 * d
         return pltpu.make_async_remote_copy(
-            src_ref=pass_y.at[stage, l],
-            dst_ref=chain_y.at[stage, l],
-            send_sem=sc_sem.at[stage, l],
-            recv_sem=rc_sem.at[stage, l],
-            device_id=(gx, gy - 2 if backward else gy + 2),
+            src_ref=pass_y.at[stage, l, pl.ds(0, 4)],
+            dst_ref=chain_y.at[stage, l, d - 1, pl.ds(0, 4)],
+            send_sem=sc_sem.at[stage, l, d - 1],
+            recv_sem=rc_sem.at[stage, l, d - 1],
+            device_id=(gx, target),
             device_id_type=MESH,
         )
 
@@ -109,11 +110,11 @@
     def x_gets(d, backward):
         return gx + d < nx if backward else gx >= d
 
-    def c_sends(backward):
-        return outer > 0 if backward else outer < half - 1
-
-    def c_gets(backward):
-        return outer < half - 1 if backward else outer > 0
+    def c_sends(d, backward):
+        return outer >= d if backward else outer + d < half
+
+    def c_gets(d, backward):
+        return outer + d < half if backward else outer >= d
 
     def start_x(l, value, rep, backward):
         back = int(backward)
@@ -133,6 +134,13 @@
             @pl.when(x_sends(d, backward))
             def _():
                 x_copy(l, stage, d, backward).start()
+        for b in range(nb):
+            field[l, b * BX:(b + 1) * BX] = value[b * BX:(b + 1) * BX]
+
+    def middle_x(l, backward):
+        back = int(backward)
+        wide = jnp.concatenate([field[l, b * BX:(b + 1) * BX] for b in range(nb)], 1)
+        high, low = split(wide)
         th = txh[back, l]
         inside[l] = dot(th, high) + dot(th, low) + dot(txl[back, l], high)
 
@@ -165,6 +173,11 @@
         both = dot(ends, pair, 1, 1)
         end_y[stage, l] = both[:8] + both[8:]
         p_copy(l, stage).start()
+        field[l] = value
+
+    def middle_y(l, backward):
+        back = int(backward)
+        pair = jnp.concatenate(split(field[l]), 1)
         wide = dot(pair, wy[back, l])
         field[l] = wide[:, :cols] + wide[:, cols:]
 
@@ -176,29 +189,36 @@
         is_first = inner == (1 if backward else 0)
         first = jnp.where(is_first, own, other)
         second = jnp.where(is_first, other, own)
-        joint = advance(first, coef_y, l, 0) + second
-
-        @pl.when(c_gets(backward))
-        def _():
-            c_copy(l, stage, backward).wait_recv()
-
-        come = chain_y[stage, l]
-        pass_y[stage, l] = advance(come, coef_y, l, 1) + joint
-
-        @pl.when(c_sends(backward))
-        def _():
-            c_copy(l, stage, backward).start()
-
-        carry_y[l] = jnp.where(is_first, come, advance(come, coef_y, l, 0) + other)
+        pass_y[stage, l] = advance(first, coef_y, l, 0) + second
+        for d in range(1, half):
+            @pl.when(c_sends(d, backward))
+            def _():
+                c_copy(l, stage, d, backward).start()
 
     def fin_y(l, rep, backward):
         back = int(backward)
-        value = field[l] + dot(three(carry_y[l]), ry[back, l], 0, 0)
+        stage = 2 * rep + back
+        for d in range(1, half):
+            @pl.when(c_gets(d, backward))
+            def _():
+                c_copy(l, stage, d, backward).wait_recv()
+        come = chain_y[stage, l, 0]
+        for d in range(2, half):
+            come += advance(chain_y[stage, l, d - 1], coef_y, l, d - 1)
+        is_first = inner == (1 if backward else 0)
+        carry = jnp.where(is_first, come, advance(come, coef_y, l, 0) + got_y[stage, l])
+        value = field[l] + dot(three(carry), ry[back, l], 0, 0)
         return value * sea[l].astype(f32)
 
     def each(body):
         lax.fori_loop(0, levels, lambda l, c: (body(l), c)[1], 0, unroll=UNROLL)
 
+    incoming = [
+        pltpu.make_async_copy(src, dst, in_sem.at[n])
+        for n, (src, dst) in enumerate(((inc_hbm, field), (dev_hbm, dev), (sea_hbm, sea)))
+    ]
+    for copy in incoming:
+        copy.start()
     side = 128
     lags = (
         lax.broadcasted_iota(jnp.int32, (side, side), 0) - lax.broadcasted_iota(jnp.int32, (side, side), 1)
@@ -263,28 +283,25 @@
             wy[back, l, lower, upper] = low
             wy[back, l, upper, upper] = zero
         ends(fy, ry, l, cols, rate, weight)
-        coefs(coef_y, l, [float(cols), 2.0 * cols], rate, weight)
+        coefs(coef_y, l, [float(cols)] + [2.0 * cols * d for d in range(1, half - 1)], rate, weight)
 
     got_x[...] = jnp.zeros_like(got_x)
+    got_y[...] = jnp.zeros_like(got_y)
     chain_y[...] = jnp.zeros_like(chain_y)
     barrier = pltpu.get_barrier_semaphore()
     for d in range(1, nx):
         pl.semaphore_signal(barrier, inc=1, device_id=(lax.rem(gx + d, nx), gy), device_id_type=MESH)
     pl.semaphore_signal(barrier, inc=1, device_id=(gx, partner), device_id_type=MESH)
-
-    @pl.when(outer > 0)
-    def _():
-        pl.semaphore_signal(barrier, inc=1, device_id=(gx, gy - 2), device_id_type=MESH)
-
-    @pl.when(outer < half - 1)
-    def _():
-        pl.semaphore_signal(barrier, inc=1, device_id=(gx, gy + 2), device_id_type=MESH)
-
+    for d in range(1, half):
+        pl.semaphore_signal(barrier, inc=1, device_id=(gx, lax.rem(gy + 2 * d, ny)), device_id_type=MESH)
     lax.fori_loop(0, levels, lambda l, c: (build(l), c)[1], 0)
-    pl.semaphore_wait(barrier, nx + jnp.minimum(outer, 1) + jnp.minimum(half - 1 - outer, 1))
+    pl.semaphore_wait(barrier, nx + half - 1)
+
+    for copy in incoming:
+        copy.wait()
 
     def begin(l):
-        value = dev[l] * sea[l].astype(f32) * inc[l]
+        value = dev[l] * sea[l].astype(f32) * field[l]
         out[l] = jnp.zeros_like(value)
         start_x(l, value, 0, False)
 
@@ -297,11 +314,17 @@
         return value
 
     def repetition(rep, c):
+        def pairs(l, backward):
+            relay_y(l, rep, backward)
+            middle_y(l, backward)
+
+        each(lambda l: middle_x(l, False))
         each(lambda l: start_x(l, fin_x(l, rep, False), rep, True))
+        each(lambda l: middle_x(l, True))
         each(lambda l: start_y(l, fin_x(l, rep, True), rep, False))
-        each(lambda l: relay_y(l, rep, False))
+        each(lambda l: pairs(l, False))
         each(lambda l: start_y(l, fin_y(l, rep, False), rep, True))
-        each(lambda l: relay_y(l, rep, True))
+        each(lambda l: pairs(l, True))
 
         @pl.when(rep < MAXSTEPS - 1)
         def _():
@@ -325,9 +348,10 @@
                         x_copy(l, stage, d, backward).wait_send()
                 p_copy(l, stage).wait_send()
 
-                @pl.when(c_sends(backward))
-                def _():
-                    c_copy(l, stage, backward).wait_send()
+                for d in range(1, half):
+                    @pl.when(c_sends(d, backward))
+                    def _():
+                        c_copy(l, stage, d, backward).wait_send()
 
     lax.fori_loop(0, levels, lambda l, c: (drain(l), c)[1], 0)
 
@@ -337,13 +361,14 @@
     nb = rows // BX
     gains = section_gain(jnp.stack([zonal_rate, meridional_rate]), filter_steps[None])
     smem = pl.BlockSpec(memory_space=pltpu.SMEM)
+    hbm = pl.BlockSpec(memory_space=pltpu.HBM)
     vmem = pl.BlockSpec(memory_space=pltpu.VMEM)
     stages = 2 * MAXSTEPS
     dma = pltpu.SemaphoreType.DMA
     return pl.pallas_call(
         functools.partial(kernel, nx, ny, levels, rows, cols),
         out_shape=jax.ShapeDtypeStruct(increment.shape, f32),
-        in_specs=[smem] * 4 + [vmem] * 3,
+        in_specs=[smem] * 4 + [hbm] * 3,
         out_specs=vmem,
         scratch_shapes=[
             pltpu.VMEM((2, levels, BX, BX), bf16),
@@ -354,7 +379,7 @@
             pltpu.VMEM((2, levels, 16, cols), bf16),
             pltpu.VMEM((2, levels, 32, cols), bf16),
             pltpu.VMEM((levels, 4 * (nx - 1), 8, 128), f32),
-            pltpu.VMEM((levels, 8, 8, 128), f32),
+            pltpu.VMEM((levels, 4 * (ny // 2 - 1), 8, 128), f32),
             pltpu.VMEM((levels, rows, cols), f32),
             pltpu.VMEM((levels, BX, nb * cols), f32),
             pltpu.VMEM((levels, 8, nb * cols), f32),
@@ -363,14 +388,16 @@
             pltpu.VMEM((stages, levels, 8, rows), f32),
             pltpu.VMEM((stages, levels, 8, rows), f32),
             pltpu.VMEM((stages, levels, 8, rows), f32),
-            pltpu.VMEM((stages, levels, 8, rows), f32),
-            pltpu.VMEM((levels, 8, rows), f32),
+            pltpu.VMEM((stages, levels, ny // 2 - 1, 8, rows), f32),
+            pltpu.VMEM((levels, rows, cols), f32),
+            pltpu.VMEM((levels, rows, cols), jnp.int32),
             dma((stages, levels, nx - 1)),
             dma((stages, levels, nx - 1)),
             dma((stages, levels)),
             dma((stages, levels)),
-            dma((stages, levels)),
-            dma((stages, levels)),
+            dma((stages, levels, ny // 2 - 1)),
+            dma((stages, levels, ny // 2 - 1)),
+            dma((3,)),
         ],
         compiler_params=pltpu.CompilerParams(
             collective_id=0, has_side_effects=True, vmem_limit_bytes=40 * 1024 * 1024

time: 100 us -> 72.5 us (0.72)
  Pallas kernels: 90.4 us -> 62.8 us
    pallas_call x1, Pallas kernels: 90.4 us -> 62.8 us  [on_device(): pl.pallas_call(functools.partial(kernel, nx, ny, levels, rows, cols), out...]
where the time goes in v3:
time: 72.5 us; the launch traced here: 72.2 us
  Pallas kernels  62.8 us (87%)
  local copies, waits for them, and re-layouts  8.05 us (11%)
  other arithmetic  1.37 us (2%)
    pallas_call x1, Pallas kernels, on_device(): pl.pallas_call(functools.partial(kernel, nx, ny, levels, rows, cols), out...  62.8 us
    unnamed x13, local copies, waits for them, and re-layouts  8.05 us

profile of v3, /device:TPU:0, one launch (start us, length us, event | category | flops | bytes accessed | tf_op | source)
XLA Modules:
  0.0 72.2 jit_solution(18021502703788106103)
XLA Ops:
  0.0 0.7 divide_subtract_fusion
  0.7 0.7 fusion.3.gains
  1.4 0.0 copy-start
  1.4 1.6 %copy-done = f32[8,512,128]{2,1,0:T(8,128)S(1)} copy-done((f32[8,512,128]{2,1,0:T(8,128)S(1)}, f32[8,512,128]{2,1,0:T(8,128)}, u32[]{:S(2)}) %copy-start) | copy-done | bytes 2097176
  3.0 0.0 copy-start.1
  3.0 1.6 %copy-done.1 = f32[8,512,128]{2,1,0:T(8,128)S(1)} copy-done((f32[8,512,128]{2,1,0:T(8,128)S(1)}, f32[8,512,128]{2,1,0:T(8,128)}, u32[]{:S(2)}) %copy-start.1) | copy-done | bytes 2097176
  4.6 0.0 copy-start.2
  4.6 1.6 %copy-done.2 = s32[8,512,128]{2,1,0:T(8,128)S(1)} copy-done((s32[8,512,128]{2,1,0:T(8,128)S(1)}, s32[8,512,128]{2,1,0:T(8,128)}, u32[]{:S(2)}) %copy-start.2) | copy-done | bytes 2097176
  6.2 0.0 copy-start.3
  6.2 0.7 copy-done.3
  6.8 0.0 copy-start.4
  6.8 0.7 copy-done.4
  7.5 0.0 copy-start.5
  7.5 0.7 copy-done.5
  8.1 62.8 %shard_map.64 = f32[8,512,128]{2,1,0:T(8,128)S(1)} custom-call(s32[8]{0:T(128)S(1)} %copy-done.5, f32[8]{0:T(128)S(1)} %copy-done.3, f32[8]{0:T(128)S(1)} %copy-done.4, f32[2,8]{1,0:T(2,128)S(1)} %fusion.3.gains, f32[8,512,128]{2,1,0:T(8,128)S(1)} %copy-done, f32[8,512,128]{2,1,0:T(8,128)S(1)} %copy-done.1, s32[8,512,128]{2,1,0:T(8,128)S(1)} %copy-done.2), custom_call_target="tpu_custom_call" | custom-call | tf_op jit(solution)/shard_map/pallas_call | solution.py:368
  70.9 1.3 %copy.8 = f32[8,512,128]{2,1,0:T(8,128)} copy(f32[8,512,128]{2,1,0:T(8,128)S(1)} %shard_map.64) | data formatting | bytes 4194304
Async XLA Ops:
  1.4 1.6 %copy-start = (f32[8,512,128]{2,1,0:T(8,128)S(1)}, f32[8,512,128]{2,1,0:T(8,128)}, u32[]{:S(2)}) copy-start(f32[8,512,128]{2,1,0:T(8,128)} %inc_hbm.1) | copy-start | bytes 6291460
  3.0 1.6 %copy-start.1 = (f32[8,512,128]{2,1,0:T(8,128)S(1)}, f32[8,512,128]{2,1,0:T(8,128)}, u32[]{:S(2)}) copy-start(f32[8,512,128]{2,1,0:T(8,128)} %dev_hbm.1) | copy-start | bytes 6291460
  4.6 1.6 %copy-start.2 = (s32[8,512,128]{2,1,0:T(8,128)S(1)}, s32[8,512,128]{2,1,0:T(8,128)}, u32[]{:S(2)}) copy-start(s32[8,512,128]{2,1,0:T(8,128)} %sea_hbm.1) | copy-start | bytes 6291460
  6.2 0.7 copy-start.3
  6.8 0.7 copy-start.4
  7.5 0.7 copy-start.5
